TPU v7x, 32 devices: a whole 2x2x4 slice. The times are simulated.
32 devices in a mesh: dp: 8 (over y, x, core), tensor: 4 (over z).
Axes of the slice: x: 2, y: 2, z: 4, core: 2. Of those that a mesh axis runs over, the one named last changes fastest.
Arguments:
- acts: bfloat16 [3072, 4096], P('dp', 'tensor'), may hold values from -6 to 6
- grad_out: bfloat16 [3072, 4096], P('dp', 'tensor'), may hold values from -60 to 60
- gate_pre: bfloat16 [3072, 14336], P('dp', 'tensor'), may hold values from -6 to 6
- up_pre: bfloat16 [3072, 14336], P('dp', 'tensor'), may hold values from -6 to 6
- down_weight: bfloat16 [14336, 4096], P('tensor', 'dp'), may hold values from -0.09375 to 0.09375
- proj_in: bfloat16 [4096, 64], P('tensor'), may hold values from -0.09375 to 0.09375
- proj_out: bfloat16 [14336, 64], P('tensor'), may hold values from -0.046875 to 0.046875
- lengths: int32 [24], P('dp'), may hold values from 64 to 128
- query_ids: int32 [16], replicated, may hold values from 0 to 23
Outputs:
- gram: float32 [4096, 4096], P('dp', 'tensor')
- scores: float32 [16, 24], P(None, 'dp')
Inputs may be any that keep to these rules, and one draw needn't show every extreme that they name: `query_ids`: queries may repeat.
All inputs are finite; a program needn't handle non-finite values.
Results may differ from a plain program's by a relative error of at most 0.004.
Values may be sent and summed in bfloat16 or wider, within the bound.
A program may use at most 128 MiB of HBM per device.

v0:
```python
import jax
import jax.numpy as jnp
from jax import lax
from jax.sharding import PartitionSpec as P


def silu_slope(value):
    sigma = jax.nn.sigmoid(value)
    return sigma + value * sigma * (1.0 - sigma)


def body(acts, grad_out, gate_pre, up_pre, down_weight, proj_in, proj_out, lengths, query_ids):
    highest = lax.Precision.HIGHEST
    tokens_here = acts.shape[0]
    examples_here = lengths.shape[0]
    seq_len = tokens_here // examples_here
    full_grad = lax.all_gather(grad_out, "tensor", axis=1, tiled=True)
    hidden_grad = lax.dot_general(
        full_grad,
        lax.all_gather(down_weight, "dp", axis=1, tiled=True),
        (((1,), (1,)), ((), ())),
        preferred_element_type=jnp.float32,
    )
    gate_value = gate_pre.astype(jnp.float32)
    gate_grad = (hidden_grad * up_pre.astype(jnp.float32) * silu_slope(gate_value)).astype(
        jnp.bfloat16
    )
    out_part = jnp.dot(gate_grad, proj_out, preferred_element_type=jnp.float32)
    in_part = jnp.dot(acts, proj_in, preferred_element_type=jnp.float32)
    out_factor, in_factor = lax.psum((out_part, in_part), "tensor")
    positions = lax.broadcasted_iota(jnp.int32, (examples_here, seq_len), 1)
    live = (positions < lengths[:, None]).astype(jnp.float32)
    out_factor = out_factor.reshape(examples_here, seq_len, -1) * live[:, :, None]
    in_factor = in_factor.reshape(examples_here, seq_len, -1)
    features = jnp.einsum("esa,esb->eab", out_factor, in_factor, precision=highest).reshape(
        examples_here, -1
    )
    width = features.shape[1]
    first_example = lax.axis_index("dp") * examples_here
    example_ids = first_example + lax.broadcasted_iota(jnp.int32, (1, examples_here), 1)
    selector = (query_ids[:, None] == example_ids).astype(jnp.float32)
    query_part = jnp.dot(selector, features, precision=highest)
    local_square = jnp.sum(features * features)
    query_feat, total_square = lax.psum((query_part, local_square), "dp")
    examples_all = examples_here * lax.axis_size("dp")
    norm_mean = total_square / examples_all + 1e-06
    col_width = width // lax.axis_size("tensor")
    own_cols = lax.dynamic_slice_in_dim(
        features, lax.axis_index("tensor") * col_width, col_width, 1
    )
    row_block = lax.all_to_all(features, "dp", split_axis=1, concat_axis=0, tiled=True)
    block = lax.dot_general(
        row_block,
        lax.all_gather(own_cols, "dp", axis=0, tiled=True),
        (((0,), (0,)), ((), ())),
        precision=highest,
        preferred_element_type=jnp.float32,
    )
    gram = block * (width / examples_all) / norm_mean
    scores = jnp.dot(query_feat, features.T, precision=highest) / norm_mean
    return (gram, scores)


def solution(mesh):
    in_specs = (
        P("dp", "tensor"),
        P("dp", "tensor"),
        P("dp", "tensor"),
        P("dp", "tensor"),
        P("tensor", "dp"),
        P("tensor", None),
        P("tensor", None),
        P("dp"),
        P(),
    )
    out_specs = (P("dp", "tensor"), P(None, "dp"))
    return jax.shard_map(body, mesh=mesh, in_specs=in_specs, out_specs=out_specs, check_vma=False)
```

profile of v0, /device:TPU:6, one launch (start us, length us, event | category | flops | bytes accessed | tf_op | source)
XLA Modules:
  0.0 371.5 jit_solution(14562197754892564738)
XLA Ops:
  7.2 0.0 copy-start
  7.2 0.0 copy-start.1
  7.2 0.0 copy-start.4
  7.2 0.0 all-gather.4.cloned.1.call-start
  7.2 0.7 all-gather.4.cloned.1.call-update
  7.9 0.0 all-gather.6.cloned.1.call-start
  8.0 0.7 all-gather.6.cloned.1.call-update
  8.7 0.0 all-reduce.6.cloned.1.call-start
  8.8 0.4 convolution_bitcast_fusion
  9.1 0.6 copy.25
  9.8 64.4 %all-gather.4.cloned.1.call-done = bf16[384,4096]{1,0:T(8,128)(2,1)} async-done(((bf16[384,1024]{1,0:T(8,128)(2,1)}), bf16[384,4096]{1,0:T(8,128)(2,1)}) %all-gather.4.cloned.1.call-update) | async-done | bytes 3145744 | tf_op jit(solution)/shard_map/all_gather | solution.py:17
  74.2 148.4 %all-gather.6.cloned.1.call-done = bf16[3584,4096]{1,0:T(8,128)(2,1)} async-done(((bf16[3584,512]{1,0:T(8,128)(2,1)}), bf16[3584,4096]{1,0:T(8,128)(2,1)}) %all-gather.6.cloned.1.call-update) | async-done | bytes 29360144 | tf_op jit(solution)/shard_map/all_gather | solution.py:20
  222.6 20.3 %fusion.9 = f32[384,64]{0,1:T(8,128)S(1)} fusion(bf16[3584,64]{0,1:T(8,128)(2,1)S(1)} %copy-done.4, bf16[384,4096]{1,0:T(8,128)(2,1)} %all-gather.4.cloned.1.call-done, bf16[3584,4096]{1,0:T(8,128)(2,1)} %all-gather.6.cloned.1.call-done, bf16[384,3584]{1,0:T(8,128)(2,1)} %param.11, bf16[384,3584]{1,0:T(8,128)(2,1)} %param.12), kind=kOutput, calls=%fused_computation.17 | convolution fusion | flops 11466964992 | bytes 38567936 | tf_op jit(solution)/shard_map/dot_general | solution.py:28
  243.0 0.7 reshape.43
  243.6 0.0 all-reduce.6.cloned.1.call-update
  243.7 0.1 fusion.14
  243.8 36.2 %all-reduce.6.cloned.1.call-done = (f32[3,128,64]{1,2,0:T(8,128)}, f32[3,128,64]{1,0,2:T(4,128)}) async-done(((f32[3,128,64]{1,2,0:T(8,128)}, f32[3,128,64]{1,0,2:T(4,128)}), (f32[3,128,64]{1,2,0:T(8,128)}, f32[3,128,64]{1,0,2:T(4,128)})) %all-reduce.6.cloned.1.call-update) | async-done | bytes 196624 | tf_op jit(solution)/shard_map/psum | solution.py:30
  280.0 0.9 broadcast_multiply_fusion
  280.9 1.8 multiply_reduce_fusion
  282.7 0.1 all_to_all.14
  282.8 0.1 reshape.45
  282.9 0.7 copy.18
  283.6 4.2 %all-to-all-start = ((f32[3,8,512]{2,0,1:T(4,128)}), f32[3,8,512]{2,0,1:T(4,128)S(1)}, u32[]{:S(2)}, u32[]{:S(2)}) async-start(f32[3,8,512]{2,0,1:T(4,128)} %copy.18), calls=%async_computation | async-start | bytes 131072 | tf_op jit(solution)/shard_map/all_to_all | solution.py:51
  287.8 1.0 fusion.10
  288.8 11.0 %psum.30 = f32[]{:T(128)} all-reduce(f32[]{:T(128)} %get-tuple-element.4), channel_id=1, replica_groups=mesh['dp'=8,'tensor'=4] {'dp'}, use_global_device_ids=true, to_apply=%region_3.0 | all-reduce | flops 1 | bytes 8 | tf_op jit(solution)/shard_map/psum | solution.py:44
  299.8 10.8 %all-gather = f32[8,3,1024]{2,1,0:T(4,128)S(1)} all-gather(f32[1,3,1024]{2,1,0:T(4,128)S(1)} %dynamic-slice_bitcast_fusion), channel_id=1, replica_groups=mesh['dp'=8,'tensor'=4] {'dp'}, dimensions={0}, use_global_device_ids=true | all-gather | bytes 110592 | tf_op jit(solution)/shard_map/all_gather | solution.py:54
  310.6 0.1 reshape.47
  310.7 0.0 all-reduce.4.cloned.1.call-update
  311.4 0.0 all-to-all-done
  311.4 3.2 multiply_divide_fusion
  314.6 48.4 %all-reduce.4.cloned.1.call-done = f32[16,4096]{1,0:T(8,128)} async-done(((f32[16,4096]{1,0:T(8,128)}), f32[16,4096]{1,0:T(8,128)}) %all-reduce.4.cloned.1.call-update) | async-done | bytes 262160 | tf_op jit(solution)/shard_map/psum | solution.py:44
  363.0 2.0 convolution_divide_fusion
  (11 shorter events, 0.0 us)
Async XLA Ops:
  7.2 1.6 copy-start
  7.2 1.6 copy-start.1
  7.2 215.4 %copy-start.4 = (bf16[3584,64]{0,1:T(8,128)(2,1)S(1)}, bf16[3584,64]{0,1:T(8,128)(2,1)}, u32[]{:S(2)}) copy-start(bf16[3584,64]{0,1:T(8,128)(2,1)} %param.15) | copy-start | bytes 1376260
  7.2 67.0 %all-gather.4.cloned.1.call-start = ((), (), s32[]{:S(2)}) async-start(), calls=%async_computation.1 | async-start | bytes 3932160 | tf_op jit(solution)/shard_map/all_gather | solution.py:17
  7.9 214.7 %all-gather.6.cloned.1.call-start = ((), (), s32[]{:S(2)}) async-start(), calls=%async_computation.2 | async-start | bytes 33030144 | tf_op jit(solution)/shard_map/all_gather | solution.py:20
  8.7 271.3 %all-reduce.6.cloned.1.call-start = ((), (), s32[]{:S(2)}) async-start(), calls=%async_computation.4 | async-start | bytes 458752 | tf_op jit(solution)/shard_map/psum | solution.py:30
  9.8 233.9 %copy-start.3 = (s32[3]{0:T(128)S(1)}, s32[3]{0:T(128)}, u32[]{:S(2)}) copy-start(s32[3]{0:T(128)} %param.16) | copy-start | bytes 40
  9.8 278.0 %copy-start.2 = (s32[16]{0:T(128)S(1)}, s32[16]{0:T(128)}, u32[]{:S(2)}) copy-start(s32[16]{0:T(128)} %param.17) | copy-start | bytes 196
  283.6 27.8 %all-to-all-start = ((f32[3,8,512]{2,0,1:T(4,128)}), f32[3,8,512]{2,0,1:T(4,128)S(1)}, u32[]{:S(2)}, u32[]{:S(2)}) async-start(f32[3,8,512]{2,0,1:T(4,128)} %copy.18), calls=%async_computation | async-start | bytes 131072 | tf_op jit(solution)/shard_map/all_to_all | solution.py:51
  287.8 75.2 %all-reduce.4.cloned.1.call-start = ((), (), s32[]{:S(2)}) async-start(), calls=%async_computation.3 | async-start | bytes 524288 | tf_op jit(solution)/shard_map/psum | solution.py:44
Sparse Core Ops, SparseCore 0:
  9.6 64.6 all-gather.3
  76.1 146.4 all-gather.5
  243.8 36.1 all-reduce.5
  310.8 52.1 all-reduce.3
where the time goes:
time: 375 us; the launch traced here: 372 us
  waiting for transfers between devices  299 us (80%)
  matrix products  28.7 us (8%)
  blocking collectives  21.8 us (6%)
  between operations  14.5 us (4%)
  starting transfers between devices  4.31 us (1%)
    all_gather x1, waiting for transfers between devices, body(): lax.all_gather(down_weight, 'dp', axis=1, tiled=True)  148 us
    all_gather x1, waiting for transfers between devices, body(): full_grad = lax.all_gather(grad_out, 'tensor', axis=1, tiled=True)  64.4 us
    psum x1, waiting for transfers between devices, body(): query_feat, total_square = lax.psum((query_part, local_square), 'dp')  48.4 us
    psum x1, waiting for transfers between devices, body(): out_factor, in_factor = lax.psum((out_part, in_part), 'tensor')  36.2 us
    dot_general x1, matrix products, body(): out_part = jnp.dot(gate_grad, proj_out, preferred_element_type=jnp.float32)  20.3 us
    psum x1, blocking collectives, body(): query_feat, total_square = lax.psum((query_part, local_square), 'dp')  11 us
    all_gather x1, blocking collectives, body(): lax.all_gather(own_cols, 'dp', axis=0, tiled=True)  10.8 us
  transfers between devices with their start and end apart: 5, of which 4 were waited for; matrix products, arithmetic and copies ran while one was open for 1% of the time, Pallas kernels for 0%

commit v1 on v0

v1 whole, which is shorter than its diff:
```python
import functools

import jax
import jax.numpy as jnp
from jax import lax
from jax.experimental import pallas as pl
from jax.experimental.pallas import tpu as pltpu
from jax.sharding import PartitionSpec as P

MESH = pl.DeviceIdType.MESH
HIGHEST = lax.Precision.HIGHEST
LANES = 128
PIECES = 7


def dot_nt(a, b, precision=None):
    return lax.dot_general(
        a, b, (((1,), (1,)), ((), ())), preferred_element_type=jnp.float32, precision=precision
    )


def kernel(
    n, nt,
    acts, grad, gate, up, weight, proj_in, proj_out, lengths, query_ids,
    gram, scores,
    wbuf, gbuf, gate_v, up_v, acts_v, pin_v, pout_v, pin_t, pout_t,
    acc, oacc, orecv, iacc, irecv, inpad, fbuf, cols, kbuf, rbuf, lhs_s, rhs_s,
    local_sem, w_send, w_recv, s_send, s_recv, g_send, g_recv, i_send, i_recv,
    o_send, o_recv, f_send, f_recv, k_send, k_recv, r_send, r_recv,
):
    me = lax.axis_index("dp")
    t = lax.axis_index("tensor")
    chips = n // 2
    half_ring = chips // 2
    chip = me // 2
    core = me % 2
    ff, kw = weight.shape
    tokens, gw = grad.shape
    ex = lengths.shape[0]
    seq = tokens // ex
    ki = proj_in.shape[1]
    ko = proj_out.shape[1]
    tiles = cols.shape[0]
    every = cols.shape[1]
    row_tiles = rbuf.shape[0]
    rows = ff // PIECES
    sibling = chip * 2 + 1 - core

    def step_left(c, s):
        if chips == 4:
            return [c, (3 * c + 2) % 5, 3 - c, (2 * c + 1) % 5][s % 4]
        return (c - s + chips) % chips

    def step_right(c, s):
        return step_left(c, chips - s)

    barrier = pltpu.get_barrier_semaphore()
    for k in range(1, n):
        pl.semaphore_signal(barrier, inc=1, device_id=((me + k) % n, t), device_id_type=MESH)
    for k in range(1, nt):
        pl.semaphore_signal(barrier, inc=1, device_id=(me, (t + k) % nt), device_id_type=MESH)
    pl.semaphore_wait(barrier, n + nt - 2)

    def remote(src, dst, send, recv, dp_id, t_id):
        return pltpu.make_async_remote_copy(
            src_ref=src, dst_ref=dst, send_sem=send, recv_sem=recv,
            device_id=(dp_id, t_id), device_id_type=MESH,
        )

    def span(way, s, p):
        if s < half_ring:
            return pl.ds(pl.multiple_of(p * rows, 32), rows)
        return pl.ds(pl.multiple_of(p * rows + way * (rows // 2), 32), rows // 2)

    def ring_send(way, s, p):
        origin = step_left(chip, s - 1) if way == 0 else step_right(chip, s - 1)
        target = step_right(chip, 1) if way == 0 else step_left(chip, 1)
        slot = origin * 2 + core
        part = span(way, s, p)
        src = weight.at[part] if s == 1 else wbuf.at[slot, part]
        return remote(
            src, wbuf.at[slot, part], w_send.at[way, s - 1, p], w_recv.at[way, s - 1, p],
            target * 2 + core, t,
        )

    def ring_slot(way, s):
        return (step_left(chip, s) if way == 0 else step_right(chip, s)) * 2 + core

    def ring_recv(way, s, p):
        slot = ring_slot(way, s)
        part = span(way, s, p)
        return remote(
            wbuf.at[slot, part], wbuf.at[slot, part],
            w_send.at[way, s - 1, p], w_recv.at[way, s - 1, p], sibling, t,
        )

    def sib_send(way, s, p):
        if s == 0:
            part = span(0, 0, p)
            return remote(
                weight.at[part], wbuf.at[me, part], s_send.at[0, p], s_recv.at[0, p], sibling, t
            )
        slot = ring_slot(way, s)
        part = span(way, s, p)
        at = 1 + way * half_ring + s - 1
        return remote(
            wbuf.at[slot, part], wbuf.at[slot, part], s_send.at[at, p], s_recv.at[at, p], sibling, t
        )

    def sib_recv(way, s, p):
        if s == 0:
            slot, at, part = sibling, 0, span(0, 0, p)
        else:
            slot = ring_slot(way, s) - core + 1 - core
            at = 1 + way * half_ring + s - 1
            part = span(way, s, p)
        return remote(
            wbuf.at[slot, part], wbuf.at[slot, part], s_send.at[at, p], s_recv.at[at, p], sibling, t
        )

    @pl.loop(0, PIECES)
    def _(p):
        ring_send(0, 1, p).start()
        ring_send(1, 1, p).start()

    def grad_copy(k):
        return remote(
            grad, gbuf.at[t], g_send.at[k], g_recv.at[k], me, (t + k) % nt
        )

    def grad_recv(k):
        src = (t - k + nt) % nt
        return remote(grad, gbuf.at[src], g_send.at[k], g_recv.at[k], me, (t + k) % nt)

    for k in range(1, nt):
        grad_copy(k).start()

    locals_ = [
        pltpu.make_async_copy(acts, acts_v, local_sem.at[0]),
        pltpu.make_async_copy(proj_in, pin_v, local_sem.at[1]),
        pltpu.make_async_copy(proj_out, pout_v, local_sem.at[2]),
        pltpu.make_async_copy(weight, wbuf.at[me], local_sem.at[3]),
        pltpu.make_async_copy(gate, gate_v, local_sem.at[4]),
        pltpu.make_async_copy(up, up_v, local_sem.at[5]),
        pltpu.make_async_copy(grad, gbuf.at[t], local_sem.at[6]),
    ]
    for copy in locals_:
        copy.start()

    @pl.loop(0, PIECES)
    def _(p):
        sib_send(0, 0, p).start()

    locals_[0].wait()
    locals_[1].wait()
    row_id = lax.broadcasted_iota(jnp.int32, (ki, ki), 0)
    col_id = lax.broadcasted_iota(jnp.int32, (ki, ki), 1)
    pin_t[...] = dot_nt((row_id == col_id).astype(jnp.bfloat16), pin_v[...]).astype(jnp.bfloat16)
    iacc[...] = dot_nt(pin_t[...], acts_v[...])

    def in_copy(k):
        return remote(iacc, irecv.at[k - 1], i_send.at[k], i_recv.at[k], me, (t + k) % nt)

    for k in range(1, nt):
        in_copy(k).start()
    locals_[2].wait()
    per_t = ko // nt
    row_id = lax.broadcasted_iota(jnp.int32, (ko, ko), 0)
    col_id = lax.broadcasted_iota(jnp.int32, (ko, ko), 1)
    place = (col_id // per_t) * per_t + (col_id % 2) * tiles + (col_id % per_t) // 2
    pout_t[...] = dot_nt((row_id == place).astype(jnp.bfloat16), pout_v[...]).astype(jnp.bfloat16)
    acc[...] = jnp.zeros_like(acc)
    inpad[...] = jnp.zeros_like(inpad)

    if half_ring > 1:
        @pl.loop(0, PIECES)
        def _(p):
            for s in range(1, half_ring):
                for way in (0, 1):
                    ring_recv(way, s, p).wait_recv()
                    ring_send(way, s + 1, p).start()
                    sib_send(way, s, p).start()

    for copy in locals_[3:]:
        copy.wait()
    for k in range(1, nt):
        grad_recv(k).wait_recv()
        in_copy(k).wait_recv()
    total_in = iacc[...]
    for k in range(1, nt):
        total_in = total_in + irecv[k - 1]
    inpad[0, 0:ki] = total_in
    inpad[1, ki : 2 * ki] = total_in

    @pl.loop(0, PIECES)
    def _(p):
        for way in (0, 1):
            ring_recv(way, half_ring, p).wait_recv()
            sib_send(way, half_ring, p).start()
        sib_recv(0, 0, p).wait_recv()
        for s in range(1, half_ring + 1):
            for way in (0, 1):
                sib_recv(way, s, p).wait_recv()
        here = pl.ds(pl.multiple_of(p * rows, LANES), rows)
        hidden = jnp.zeros((tokens, rows), jnp.float32)
        for j in range(n):
            at = j * kw
            hidden = hidden + dot_nt(
                gbuf[at // gw, :, at % gw : at % gw + kw], wbuf[j, here, :]
            )
        value = gate_v[:, here].astype(jnp.float32)
        sigma = jax.nn.sigmoid(value)
        slope = sigma + value * sigma * (1.0 - sigma)
        grads = (hidden * up_v[:, here].astype(jnp.float32) * slope).astype(jnp.bfloat16)
        acc[...] += dot_nt(pout_t[:, here], grads)

    for tt in range(nt):
        for par in (0, 1):
            first = (tt * 2 + par) * tiles
            oacc[tt, par] = acc[first : first + tiles, :]

    def out_copy(k):
        to = (t + k) % nt
        return remote(oacc.at[to], orecv.at[k - 1], o_send.at[k], o_recv.at[k], me, to)

    for k in range(1, nt):
        out_copy(k).start()
    for k in range(1, nt):
        out_copy(k).wait_recv()
    evens = oacc[t, 0]
    odds = oacc[t, 1]
    for k in range(1, nt):
        evens = evens + orecv[k - 1, 0]
        odds = odds + orecv[k - 1, 1]

    position = lax.broadcasted_iota(jnp.int32, (tiles, seq), 1)
    for e in range(ex):
        live = (position < lengths[e]).astype(jnp.float32)
        own = slice(e * seq, (e + 1) * seq)
        fbuf[me * ex + e] = dot_nt(evens[:, own] * live, inpad[0, :, own], HIGHEST) + dot_nt(
            odds[:, own] * live, inpad[1, :, own], HIGHEST
        )

    def feat_copy(k):
        part = fbuf.at[pl.ds(me * ex, ex)]
        return remote(part, part, f_send.at[k], f_recv.at[k], (me + k) % n, t)

    def feat_recv(k):
        part = fbuf.at[pl.ds(((me - k + n) % n) * ex, ex)]
        return remote(part, part, f_send.at[k], f_recv.at[k], (me + k) % n, t)

    for k in range(1, n):
        feat_copy(k).start()
    for k in range(1, n):
        feat_recv(k).wait_recv()

    for s in range(tiles):
        cols[s] = fbuf[:, s, :]

    owner = (me * row_tiles) // tiles
    offset = (me * row_tiles) % tiles

    def row_copy(k):
        return remote(
            cols.at[pl.ds(offset, row_tiles)], rbuf, r_send.at[k], r_recv, me, (t + k) % nt
        )

    @pl.when(t == owner)
    def _():
        for k in range(1, nt):
            row_copy(k).start()
        rbuf[...] = cols[pl.ds(offset, row_tiles)]

    inner = jnp.zeros((every, every), jnp.float32)
    for s in range(tiles):
        inner = inner + dot_nt(cols[s], cols[s], HIGHEST)
    kbuf[t] = jnp.zeros(kbuf.shape[1:], jnp.float32)
    kbuf[t, :, 0:every] = inner

    def inner_copy(k):
        return remote(kbuf.at[t], kbuf.at[t], k_send.at[k], k_recv.at[k], me, (t + k) % nt)

    def inner_recv(k):
        src = (t - k + nt) % nt
        return remote(kbuf.at[src], kbuf.at[src], k_send.at[k], k_recv.at[k], me, (t + k) % nt)

    for k in range(1, nt):
        inner_copy(k).start()

    for s in range(tiles):
        value = cols[s]
        high = value.astype(jnp.bfloat16).astype(jnp.float32)
        own = slice(s * LANES, (s + 1) * LANES)
        rhs_s[0:every, own] = high
        rhs_s[every : 2 * every, own] = value - high
        rhs_s[2 * every : 3 * every, own] = high
    right = rhs_s[...].astype(jnp.bfloat16)

    for k in range(1, nt):
        inner_recv(k).wait_recv()
    whole = kbuf[0]
    for tt in range(1, nt):
        whole = whole + kbuf[tt]
    whole = whole[:, 0:every]
    r_id = lax.broadcasted_iota(jnp.int32, (every, every), 0)
    c_id = lax.broadcasted_iota(jnp.int32, (every, every), 1)
    norm_mean = jnp.sum(jnp.where(r_id == c_id, whole, 0.0)) / every + 1e-6

    queries = scores.shape[0]
    q_row = lax.broadcasted_iota(jnp.int32, (queries, every), 0)
    q_col = lax.broadcasted_iota(jnp.int32, (queries, every), 1)
    chosen = jnp.zeros((queries, every), jnp.float32)
    for q in range(queries):
        chosen = jnp.where((q_row == q) & (q_col == query_ids[q]), 1.0, chosen)
    picked = jnp.dot(chosen, whole, precision=HIGHEST, preferred_element_type=jnp.float32)
    e_row = lax.broadcasted_iota(jnp.int32, (ex, every), 0)
    e_col = lax.broadcasted_iota(jnp.int32, (ex, every), 1)
    mine = (e_col == e_row + me * ex).astype(jnp.float32)
    scores[...] = dot_nt(picked, mine, HIGHEST) / norm_mean

    @pl.when(t != owner)
    def _():
        row_copy(1).wait_recv()

    for s in range(row_tiles):
        value = rbuf[s]
        high = value.astype(jnp.bfloat16).astype(jnp.float32)
        own = slice(s * LANES, (s + 1) * LANES)
        lhs_s[0:every, own] = high
        lhs_s[every : 2 * every, own] = high
        lhs_s[2 * every : 3 * every, own] = value - high
    scale = (tiles * nt * LANES / every) / norm_mean
    for s in range(row_tiles):
        own = slice(s * LANES, (s + 1) * LANES)
        left = lhs_s[:, own].T.astype(jnp.bfloat16)
        gram[own, :] = jnp.dot(left, right, preferred_element_type=jnp.float32) * scale

    @pl.loop(0, PIECES)
    def _(p):
        sib_send(0, 0, p).wait_send()
        for s in range(1, half_ring + 1):
            for way in (0, 1):
                ring_send(way, s, p).wait_send()
                sib_send(way, s, p).wait_send()

    for k in range(1, nt):
        grad_copy(k).wait_send()
        in_copy(k).wait_send()
        out_copy(k).wait_send()
        inner_copy(k).wait_send()
    for k in range(1, n):
        feat_copy(k).wait_send()

    @pl.when(t == owner)
    def _():
        for k in range(1, nt):
            row_copy(k).wait_send()


def body(n, nt, acts, grad_out, gate_pre, up_pre, down_weight, proj_in, proj_out, lengths, query_ids):
    tokens, gw = grad_out.shape
    ff, kw = down_weight.shape
    ki = proj_in.shape[1]
    ko = proj_out.shape[1]
    ex = lengths.shape[0]
    every = ex * n
    width = ki * ko
    tiles = width // nt // LANES
    row_tiles = width // n // LANES
    half_ring = n // 4
    bf16, f32 = jnp.bfloat16, jnp.float32
    dma = pltpu.SemaphoreType.DMA
    hbm = pl.BlockSpec(memory_space=pl.ANY)
    smem = pl.BlockSpec(memory_space=pltpu.SMEM)
    vmem = pl.BlockSpec(memory_space=pltpu.VMEM)
    return pl.pallas_call(
        functools.partial(kernel, n, nt),
        out_shape=(
            jax.ShapeDtypeStruct((width // n, width // nt), f32),
            jax.ShapeDtypeStruct((query_ids.shape[0], ex), f32),
        ),
        in_specs=[hbm] * 7 + [smem] * 2,
        out_specs=(vmem, vmem),
        scratch_shapes=[
            pltpu.VMEM((n, ff, kw), bf16),
            pltpu.VMEM((nt, tokens, gw), bf16),
            pltpu.VMEM((tokens, ff), bf16),
            pltpu.VMEM((tokens, ff), bf16),
            pltpu.VMEM((tokens, gw), bf16),
            pltpu.VMEM((gw, ki), bf16),
            pltpu.VMEM((ff, ko), bf16),
            pltpu.VMEM((ki, gw), bf16),
            pltpu.VMEM((ko, ff), bf16),
            pltpu.VMEM((ko, tokens), f32),
            pltpu.VMEM((nt, 2, tiles, tokens), f32),
            pltpu.VMEM((nt - 1, 2, tiles, tokens), f32),
            pltpu.VMEM((ki, tokens), f32),
            pltpu.VMEM((nt - 1, ki, tokens), f32),
            pltpu.VMEM((2, 2 * ki, tokens), f32),
            pltpu.VMEM((every, tiles, LANES), f32),
            pltpu.VMEM((tiles, every, LANES), f32),
            pltpu.VMEM((nt, every, LANES), f32),
            pltpu.VMEM((row_tiles, every, LANES), f32),
            pltpu.VMEM((3 * every, row_tiles * LANES), f32),
            pltpu.VMEM((3 * every, tiles * LANES), f32),
            dma((7,)),
            dma((2, half_ring, PIECES)),
            dma((2, half_ring, PIECES)),
            dma((1 + 2 * half_ring, PIECES)),
            dma((1 + 2 * half_ring, PIECES)),
            dma((nt,)), dma((nt,)), dma((nt,)), dma((nt,)), dma((nt,)), dma((nt,)),
            dma((n,)), dma((n,)),
            dma((nt,)), dma((nt,)),
            dma((nt,)), dma,
        ],
        compiler_params=pltpu.CompilerParams(
            collective_id=0, has_side_effects=True, vmem_limit_bytes=60 * 1024 * 1024
        ),
    )(acts, grad_out, gate_pre, up_pre, down_weight, proj_in, proj_out, lengths, query_ids)


def solution(mesh):
    in_specs = (
        P("dp", "tensor"),
        P("dp", "tensor"),
        P("dp", "tensor"),
        P("dp", "tensor"),
        P("tensor", "dp"),
        P("tensor", None),
        P("tensor", None),
        P("dp"),
        P(),
    )
    out_specs = (P("dp", "tensor"), P(None, "dp"))
    return jax.shard_map(
        functools.partial(body, mesh.shape["dp"], mesh.shape["tensor"]),
        mesh=mesh, in_specs=in_specs, out_specs=out_specs, check_vma=False,
    )
```

time: 375 us -> 156 us (0.42)
  waiting for transfers between devices: 299 us -> 0 us
  Pallas kernels: 0 us -> 146 us
  matrix products: 28.7 us -> 0 us
  blocking collectives: 21.8 us -> 0 us
  between operations: 14.5 us -> 0.64 us
  local copies, waits for them, and re-layouts: 2.3 us -> 8.54 us
  starting transfers between devices: 4.31 us -> 0 us
    all_gather x2 -> x0, waiting for transfers between devices: 213 us -> none  [the longest x1 148 us: body(): lax.all_gather(down_weight, 'dp', axis=1, tiled=True)]
    pallas_call x0 -> x1, Pallas kernels: none -> 146 us  [body(): pl.pallas_call(functools.partial(kernel, n, nt), out_shape=(jax.ShapeDtyp...]
    psum x2 -> x0, waiting for transfers between devices: 84.7 us -> none  [the longest x1 48.4 us: body(): query_feat, total_square = lax.psum((query_part, local_square), 'dp')]
    dot_general x6 -> x0, matrix products: 28.7 us -> none  [the longest x1 20.3 us: body(): out_part = jnp.dot(gate_grad, proj_out, preferred_element_type=jnp.float32)]
    psum x1 -> x0, blocking collectives: 11 us -> none  [body(): query_feat, total_square = lax.psum((query_part, local_square), 'dp')]
    all_gather x1 -> x0, blocking collectives: 10.8 us -> none  [body(): lax.all_gather(own_cols, 'dp', axis=0, tiled=True)]
    unnamed x12 -> x3, local copies, waits for them, and re-layouts: 0.08 us -> 7.19 us
    all_to_all x1 -> x0, starting transfers between devices: 4.2 us -> none  [body(): lax.all_to_all(features, 'dp', split_axis=1, concat_axis=0, tiled=True)]
  transfers between devices with their start and end apart: 5 -> 0, of which waited for: 4 -> 0; matrix products, arithmetic and copies ran while one was open for 1% -> 0% of each run, Pallas kernels for 0% -> 0%
where the time goes in v1:
time: 156 us; the launch traced here: 155 us
  Pallas kernels  146 us (94%)
  local copies, waits for them, and re-layouts  8.54 us (5%)
    pallas_call x1, Pallas kernels, body(): pl.pallas_call(functools.partial(kernel, n, nt), out_shape=(jax.ShapeDtyp...  146 us
    unnamed x3, local copies, waits for them, and re-layouts  7.19 us

profile of v1, /device:TPU:6, one launch (start us, length us, event | category | flops | bytes accessed | tf_op | source)
XLA Modules:
  0.0 155.4 jit_solution(14467568739860005889)
XLA Ops:
  0.6 1.8 %copy.11.proj_in = bf16[1024,64]{1,0:T(8,128)(2,1)} copy(bf16[1024,64]{0,1:T(8,128)(2,1)} %param.14) | data formatting | bytes 262144 | tf_op args[5]
  2.4 2.3 %copy.12.proj_out = bf16[3584,64]{1,0:T(8,128)(2,1)} copy(bf16[3584,64]{0,1:T(8,128)(2,1)} %param.15) | data formatting | bytes 917504 | tf_op args[6]
  4.7 146.2 %shard_map.104 = (f32[512,1024]{1,0:T(8,128)}, f32[16,3]{1,0:T(8,128)}) custom-call(bf16[384,1024]{1,0:T(8,128)(2,1)} %acts.1, bf16[384,1024]{1,0:T(8,128)(2,1)} %grad.1, bf16[384,3584]{1,0:T(8,128)(2,1)} %gate.1, bf16[384,3584]{1,0:T(8,128)(2,1)} %up.1, bf16[3584,512]{1,0:T(8,128)(2,1)} %weight.1, bf16[1024,64]{1,0:T(8,128)(2,1)} %copy.11.proj_in, ...), custom_call_target="tpu_custom_call" | custom-call | tf_op jit(solution)/shard_map/pallas_call | solution.py:376
  150.9 1.3 copy.13
  152.2 3.2 %copy.15 = f32[512,1024]{1,0:T(8,128)} copy(f32[512,1024]{1,0:T(8,128)} %get-tuple-element.6) | data formatting | bytes 4194304

commit v2 on v1

--- a/solution.py
+++ b/solution.py
@@ -21,10 +21,10 @@
 
 def kernel(
     n, nt,
-    acts, grad, gate, up, weight, proj_in, proj_out, lengths, query_ids,
-    gram, scores,
-    wbuf, gbuf, gate_v, up_v, acts_v, pin_v, pout_v, pin_t, pout_t,
-    acc, oacc, orecv, iacc, irecv, inpad, fbuf, cols, kbuf, rbuf, lhs_s, rhs_s,
+    acts, grad, gate, up, weight, proj_in, proj_out, lengths,
+    cols, rbuf, inner_out,
+    wbuf, gbuf, gate_v, up_v, acts_v, pin_v, pout_v, pout_t,
+    acc, oacc, orecv, iacc, irecv, inpad, fbuf, kbuf,
     local_sem, w_send, w_recv, s_send, s_recv, g_send, g_recv, i_send, i_recv,
     o_send, o_recv, f_send, f_recv, k_send, k_recv, r_send, r_recv,
 ):
@@ -38,8 +38,8 @@
     tokens, gw = grad.shape
     ex = lengths.shape[0]
     seq = tokens // ex
-    ki = proj_in.shape[1]
-    ko = proj_out.shape[1]
+    ki = proj_in.shape[0]
+    ko = proj_out.shape[0]
     tiles = cols.shape[0]
     every = cols.shape[1]
     row_tiles = rbuf.shape[0]
@@ -153,10 +153,7 @@
 
     locals_[0].wait()
     locals_[1].wait()
-    row_id = lax.broadcasted_iota(jnp.int32, (ki, ki), 0)
-    col_id = lax.broadcasted_iota(jnp.int32, (ki, ki), 1)
-    pin_t[...] = dot_nt((row_id == col_id).astype(jnp.bfloat16), pin_v[...]).astype(jnp.bfloat16)
-    iacc[...] = dot_nt(pin_t[...], acts_v[...])
+    iacc[...] = dot_nt(pin_v[...], acts_v[...])
 
     def in_copy(k):
         return remote(iacc, irecv.at[k - 1], i_send.at[k], i_recv.at[k], me, (t + k) % nt)
@@ -168,7 +165,9 @@
     row_id = lax.broadcasted_iota(jnp.int32, (ko, ko), 0)
     col_id = lax.broadcasted_iota(jnp.int32, (ko, ko), 1)
     place = (col_id // per_t) * per_t + (col_id % 2) * tiles + (col_id % per_t) // 2
-    pout_t[...] = dot_nt((row_id == place).astype(jnp.bfloat16), pout_v[...]).astype(jnp.bfloat16)
+    pout_t[...] = jnp.dot(
+        (row_id == place).astype(jnp.bfloat16), pout_v[...], preferred_element_type=jnp.float32
+    ).astype(jnp.bfloat16)
     acc[...] = jnp.zeros_like(acc)
     inpad[...] = jnp.zeros_like(inpad)
 
@@ -287,53 +286,16 @@
     for k in range(1, nt):
         inner_copy(k).start()
 
-    for s in range(tiles):
-        value = cols[s]
-        high = value.astype(jnp.bfloat16).astype(jnp.float32)
-        own = slice(s * LANES, (s + 1) * LANES)
-        rhs_s[0:every, own] = high
-        rhs_s[every : 2 * every, own] = value - high
-        rhs_s[2 * every : 3 * every, own] = high
-    right = rhs_s[...].astype(jnp.bfloat16)
-
     for k in range(1, nt):
         inner_recv(k).wait_recv()
     whole = kbuf[0]
     for tt in range(1, nt):
         whole = whole + kbuf[tt]
-    whole = whole[:, 0:every]
-    r_id = lax.broadcasted_iota(jnp.int32, (every, every), 0)
-    c_id = lax.broadcasted_iota(jnp.int32, (every, every), 1)
-    norm_mean = jnp.sum(jnp.where(r_id == c_id, whole, 0.0)) / every + 1e-6
-
-    queries = scores.shape[0]
-    q_row = lax.broadcasted_iota(jnp.int32, (queries, every), 0)
-    q_col = lax.broadcasted_iota(jnp.int32, (queries, every), 1)
-    chosen = jnp.zeros((queries, every), jnp.float32)
-    for q in range(queries):
-        chosen = jnp.where((q_row == q) & (q_col == query_ids[q]), 1.0, chosen)
-    picked = jnp.dot(chosen, whole, precision=HIGHEST, preferred_element_type=jnp.float32)
-    e_row = lax.broadcasted_iota(jnp.int32, (ex, every), 0)
-    e_col = lax.broadcasted_iota(jnp.int32, (ex, every), 1)
-    mine = (e_col == e_row + me * ex).astype(jnp.float32)
-    scores[...] = dot_nt(picked, mine, HIGHEST) / norm_mean
+    inner_out[...] = whole
 
     @pl.when(t != owner)
     def _():
         row_copy(1).wait_recv()
-
-    for s in range(row_tiles):
-        value = rbuf[s]
-        high = value.astype(jnp.bfloat16).astype(jnp.float32)
-        own = slice(s * LANES, (s + 1) * LANES)
-        lhs_s[0:every, own] = high
-        lhs_s[every : 2 * every, own] = high
-        lhs_s[2 * every : 3 * every, own] = value - high
-    scale = (tiles * nt * LANES / every) / norm_mean
-    for s in range(row_tiles):
-        own = slice(s * LANES, (s + 1) * LANES)
-        left = lhs_s[:, own].T.astype(jnp.bfloat16)
-        gram[own, :] = jnp.dot(left, right, preferred_element_type=jnp.float32) * scale
 
     @pl.loop(0, PIECES)
     def _(p):
@@ -355,6 +317,48 @@
     def _():
         for k in range(1, nt):
             row_copy(k).wait_send()
+
+
+def finish(cols, rbuf, inner, query_ids, gram, scores, rhs_s, lhs_s, left_s, scale_s):
+    tiles, every = cols.shape[0], cols.shape[1]
+    step = pl.program_id(0)
+
+    @pl.when(step == 0)
+    def _():
+        for s in range(tiles):
+            value = cols[s]
+            high = value.astype(jnp.bfloat16).astype(jnp.float32)
+            own = slice(s * LANES, (s + 1) * LANES)
+            lhs_s[0:every, own] = high
+            lhs_s[every : 2 * every, own] = value - high
+            lhs_s[2 * every : 3 * every, own] = high
+        rhs_s[...] = lhs_s[...].astype(jnp.bfloat16)
+        whole = inner[:, 0:every]
+        r_id = lax.broadcasted_iota(jnp.int32, (every, every), 0)
+        c_id = lax.broadcasted_iota(jnp.int32, (every, every), 1)
+        norm_mean = jnp.sum(jnp.where(r_id == c_id, whole, 0.0)) / every + 1e-6
+        ex, queries = scores.shape
+        q_row = lax.broadcasted_iota(jnp.int32, (queries, every), 0)
+        q_col = lax.broadcasted_iota(jnp.int32, (queries, every), 1)
+        chosen = jnp.zeros((queries, every), jnp.float32)
+        for q in range(queries):
+            chosen = jnp.where((q_row == q) & (q_col == query_ids[q]), 1.0, chosen)
+        e_row = lax.broadcasted_iota(jnp.int32, (ex, every), 0)
+        e_col = lax.broadcasted_iota(jnp.int32, (ex, every), 1)
+        mine = (e_col == e_row + lax.axis_index("dp") * ex).astype(jnp.float32)
+        picked = jnp.dot(mine, whole, precision=HIGHEST, preferred_element_type=jnp.float32)
+        scores[...] = dot_nt(picked, chosen, HIGHEST) / norm_mean
+        width = tiles * LANES * lax.axis_size("tensor")
+        scale_s[0] = (width / every) / norm_mean
+
+    value = rbuf[step]
+    high = value.astype(jnp.bfloat16).astype(jnp.float32)
+    left_s[0:every, :] = high
+    left_s[every : 2 * every, :] = high
+    left_s[2 * every : 3 * every, :] = value - high
+    left = left_s[...].T.astype(jnp.bfloat16)
+    product = jnp.dot(left, rhs_s[...], preferred_element_type=jnp.float32)
+    gram[...] = product * scale_s[0]
 
 
 def body(n, nt, acts, grad_out, gate_pre, up_pre, down_weight, proj_in, proj_out, lengths, query_ids):
@@ -373,23 +377,23 @@
     hbm = pl.BlockSpec(memory_space=pl.ANY)
     smem = pl.BlockSpec(memory_space=pltpu.SMEM)
     vmem = pl.BlockSpec(memory_space=pltpu.VMEM)
-    return pl.pallas_call(
+    cols, rows, inner = pl.pallas_call(
         functools.partial(kernel, n, nt),
         out_shape=(
-            jax.ShapeDtypeStruct((width // n, width // nt), f32),
-            jax.ShapeDtypeStruct((query_ids.shape[0], ex), f32),
+            jax.ShapeDtypeStruct((tiles, every, LANES), f32),
+            jax.ShapeDtypeStruct((row_tiles, every, LANES), f32),
+            jax.ShapeDtypeStruct((every, LANES), f32),
         ),
-        in_specs=[hbm] * 7 + [smem] * 2,
-        out_specs=(vmem, vmem),
+        in_specs=[hbm] * 7 + [smem],
+        out_specs=(vmem, vmem, vmem),
         scratch_shapes=[
             pltpu.VMEM((n, ff, kw), bf16),
             pltpu.VMEM((nt, tokens, gw), bf16),
             pltpu.VMEM((tokens, ff), bf16),
             pltpu.VMEM((tokens, ff), bf16),
             pltpu.VMEM((tokens, gw), bf16),
-            pltpu.VMEM((gw, ki), bf16),
-            pltpu.VMEM((ff, ko), bf16),
             pltpu.VMEM((ki, gw), bf16),
+            pltpu.VMEM((ko, ff), bf16),
             pltpu.VMEM((ko, ff), bf16),
             pltpu.VMEM((ko, tokens), f32),
             pltpu.VMEM((nt, 2, tiles, tokens), f32),
@@ -398,11 +402,7 @@
             pltpu.VMEM((nt - 1, ki, tokens), f32),
             pltpu.VMEM((2, 2 * ki, tokens), f32),
             pltpu.VMEM((every, tiles, LANES), f32),
-            pltpu.VMEM((tiles, every, LANES), f32),
             pltpu.VMEM((nt, every, LANES), f32),
-            pltpu.VMEM((row_tiles, every, LANES), f32),
-            pltpu.VMEM((3 * every, row_tiles * LANES), f32),
-            pltpu.VMEM((3 * every, tiles * LANES), f32),
             dma((7,)),
             dma((2, half_ring, PIECES)),
             dma((2, half_ring, PIECES)),
@@ -416,7 +416,32 @@
         compiler_params=pltpu.CompilerParams(
             collective_id=0, has_side_effects=True, vmem_limit_bytes=60 * 1024 * 1024
         ),
-    )(acts, grad_out, gate_pre, up_pre, down_weight, proj_in, proj_out, lengths, query_ids)
+    )(acts, grad_out, gate_pre, up_pre, down_weight, proj_in.T, proj_out.T, lengths)
+    gram, scores = pl.pallas_call(
+        finish,
+        grid=(row_tiles,),
+        out_shape=(
+            jax.ShapeDtypeStruct((width // n, width // nt), f32),
+            jax.ShapeDtypeStruct((ex, query_ids.shape[0]), f32),
+        ),
+        in_specs=[
+            pl.BlockSpec((tiles, every, LANES), lambda i: (0, 0, 0)),
+            pl.BlockSpec((row_tiles, every, LANES), lambda i: (0, 0, 0)),
+            pl.BlockSpec((every, LANES), lambda i: (0, 0)),
+            smem,
+        ],
+        out_specs=(
+            pl.BlockSpec((LANES, width // nt), lambda i: (i, 0)),
+            pl.BlockSpec((ex, query_ids.shape[0]), lambda i: (0, 0)),
+        ),
+        scratch_shapes=[
+            pltpu.VMEM((3 * every, tiles * LANES), bf16),
+            pltpu.VMEM((3 * every, tiles * LANES), f32),
+            pltpu.VMEM((3 * every, LANES), f32),
+            pltpu.SMEM((1,), f32),
+        ],
+    )(cols, rows, inner, query_ids)
+    return gram, scores.T
 
 
 def solution(mesh):

time: 156 us -> 149 us (0.955)
  local copies, waits for them, and re-layouts: 8.54 us -> 0 us
  Pallas kernels: 146 us -> 148 us
    unnamed x3 -> x0, local copies, waits for them, and re-layouts: 7.19 us -> none
    pallas_call x0 -> x1, Pallas kernels: none -> 3.71 us  [body(): pl.pallas_call(finish, grid=(row_tiles,), out_shape=(jax.ShapeDtypeStruct...]
where the time goes in v2:
time: 149 us
  Pallas kernels  148 us (99%)
    pallas_call x1, Pallas kernels, body(): pl.pallas_call(functools.partial(kernel, n, nt), out_shape=(jax.ShapeDtyp...  145 us
    pallas_call x1, Pallas kernels, body(): pl.pallas_call(finish, grid=(row_tiles,), out_shape=(jax.ShapeDtypeStruct...  3.71 us

profile of v2, /device:TPU:6, one launch (start us, length us, event | category | flops | bytes accessed | tf_op | source)
XLA Modules:
  0.0 149.0 jit_solution(7600266862148293139)
XLA Ops:
  0.6 144.7 %shard_map.104 = (f32[8,24,128]{2,1,0:T(8,128)}, f32[4,24,128]{2,1,0:T(8,128)}, f32[24,128]{1,0:T(8,128)}) custom-call(bf16[384,1024]{1,0:T(8,128)(2,1)} %acts.1, bf16[384,1024]{1,0:T(8,128)(2,1)} %grad.1, bf16[384,3584]{1,0:T(8,128)(2,1)} %gate.1, bf16[384,3584]{1,0:T(8,128)(2,1)} %up.1, bf16[3584,512]{1,0:T(8,128)(2,1)} %weight.1, ...), custom_call_target="tpu_custom_call" | custom-call | tf_op jit(solution)/shard_map/pallas_call | solution.py:380
  145.3 3.7 %shard_map.105 = (f32[512,1024]{1,0:T(8,128)}, f32[3,16]{1,0:T(4,128)}) custom-call(f32[8,24,128]{2,1,0:T(8,128)} %get-tuple-element.7.cols, f32[4,24,128]{2,1,0:T(8,128)} %get-tuple-element.8.rbuf, f32[24,128]{1,0:T(8,128)} %get-tuple-element.9.inner, s32[16]{0:T(128)} %query_ids.1), custom_call_target="tpu_custom_call" | custom-call | tf_op jit(solution)/shard_map/pallas_call | solution.py:420

commit v3 on v2

--- a/solution.py
+++ b/solution.py
@@ -22,9 +22,9 @@
 def kernel(
     n, nt,
     acts, grad, gate, up, weight, proj_in, proj_out, lengths,
-    cols, rbuf, inner_out,
+    rhs, rbuf, inner_out,
     wbuf, gbuf, gate_v, up_v, acts_v, pin_v, pout_v, pout_t,
-    acc, oacc, orecv, iacc, irecv, inpad, fbuf, kbuf,
+    acc, oacc, orecv, iacc, irecv, inpad, fbuf, kbuf, cols, rhs_s,
     local_sem, w_send, w_recv, s_send, s_recv, g_send, g_recv, i_send, i_recv,
     o_send, o_recv, f_send, f_recv, k_send, k_recv, r_send, r_recv,
 ):
@@ -193,20 +193,30 @@
 
     @pl.loop(0, PIECES)
     def _(p):
+        here = pl.ds(pl.multiple_of(p * rows, LANES), rows)
+
+        def product(slot):
+            at = slot * kw
+            own = pl.ds(pl.multiple_of(at % gw, LANES), kw)
+            return dot_nt(gbuf[at // gw, :, own], wbuf[slot, here, :])
+
+        sib_recv(0, 0, p).wait_recv()
+        for s in range(1, half_ring):
+            for way in (0, 1):
+                sib_recv(way, s, p).wait_recv()
+        hidden = product(me) + product(sibling)
+        for s in range(1, half_ring):
+            for way in (0, 1):
+                slot = ring_slot(way, s)
+                hidden = hidden + product(slot) + product(slot - core + 1 - core)
         for way in (0, 1):
             ring_recv(way, half_ring, p).wait_recv()
             sib_send(way, half_ring, p).start()
-        sib_recv(0, 0, p).wait_recv()
-        for s in range(1, half_ring + 1):
-            for way in (0, 1):
-                sib_recv(way, s, p).wait_recv()
-        here = pl.ds(pl.multiple_of(p * rows, LANES), rows)
-        hidden = jnp.zeros((tokens, rows), jnp.float32)
-        for j in range(n):
-            at = j * kw
-            hidden = hidden + dot_nt(
-                gbuf[at // gw, :, at % gw : at % gw + kw], wbuf[j, here, :]
-            )
+        far = ring_slot(0, half_ring)
+        hidden = hidden + product(far)
+        for way in (0, 1):
+            sib_recv(way, half_ring, p).wait_recv()
+        hidden = hidden + product(far - core + 1 - core)
         value = gate_v[:, here].astype(jnp.float32)
         sigma = jax.nn.sigmoid(value)
         slope = sigma + value * sigma * (1.0 - sigma)
@@ -285,6 +295,15 @@
 
     for k in range(1, nt):
         inner_copy(k).start()
+
+    for s in range(tiles):
+        value = cols[s]
+        high = value.astype(jnp.bfloat16).astype(jnp.float32)
+        own = slice(s * LANES, (s + 1) * LANES)
+        rhs_s[0:every, own] = high
+        rhs_s[every : 2 * every, own] = value - high
+        rhs_s[2 * every : 3 * every, own] = high
+    rhs[...] = rhs_s[...].astype(jnp.bfloat16)
 
     for k in range(1, nt):
         inner_recv(k).wait_recv()
@@ -319,20 +338,12 @@
             row_copy(k).wait_send()
 
 
-def finish(cols, rbuf, inner, query_ids, gram, scores, rhs_s, lhs_s, left_s, scale_s):
-    tiles, every = cols.shape[0], cols.shape[1]
+def finish(rhs, rbuf, inner, query_ids, gram, scores, left_s, scale_s):
+    every = inner.shape[0]
     step = pl.program_id(0)
 
     @pl.when(step == 0)
     def _():
-        for s in range(tiles):
-            value = cols[s]
-            high = value.astype(jnp.bfloat16).astype(jnp.float32)
-            own = slice(s * LANES, (s + 1) * LANES)
-            lhs_s[0:every, own] = high
-            lhs_s[every : 2 * every, own] = value - high
-            lhs_s[2 * every : 3 * every, own] = high
-        rhs_s[...] = lhs_s[...].astype(jnp.bfloat16)
         whole = inner[:, 0:every]
         r_id = lax.broadcasted_iota(jnp.int32, (every, every), 0)
         c_id = lax.broadcasted_iota(jnp.int32, (every, every), 1)
@@ -348,7 +359,7 @@
         mine = (e_col == e_row + lax.axis_index("dp") * ex).astype(jnp.float32)
         picked = jnp.dot(mine, whole, precision=HIGHEST, preferred_element_type=jnp.float32)
         scores[...] = dot_nt(picked, chosen, HIGHEST) / norm_mean
-        width = tiles * LANES * lax.axis_size("tensor")
+        width = rhs.shape[1] * lax.axis_size("tensor")
         scale_s[0] = (width / every) / norm_mean
 
     value = rbuf[step]
@@ -357,7 +368,7 @@
     left_s[every : 2 * every, :] = high
     left_s[2 * every : 3 * every, :] = value - high
     left = left_s[...].T.astype(jnp.bfloat16)
-    product = jnp.dot(left, rhs_s[...], preferred_element_type=jnp.float32)
+    product = jnp.dot(left, rhs[...], preferred_element_type=jnp.float32)
     gram[...] = product * scale_s[0]
 
 
@@ -377,10 +388,10 @@
     hbm = pl.BlockSpec(memory_space=pl.ANY)
     smem = pl.BlockSpec(memory_space=pltpu.SMEM)
     vmem = pl.BlockSpec(memory_space=pltpu.VMEM)
-    cols, rows, inner = pl.pallas_call(
+    rhs, rows, inner = pl.pallas_call(
         functools.partial(kernel, n, nt),
         out_shape=(
-            jax.ShapeDtypeStruct((tiles, every, LANES), f32),
+            jax.ShapeDtypeStruct((3 * every, tiles * LANES), bf16),
             jax.ShapeDtypeStruct((row_tiles, every, LANES), f32),
             jax.ShapeDtypeStruct((every, LANES), f32),
         ),
@@ -403,6 +414,8 @@
             pltpu.VMEM((2, 2 * ki, tokens), f32),
             pltpu.VMEM((every, tiles, LANES), f32),
             pltpu.VMEM((nt, every, LANES), f32),
+            pltpu.VMEM((tiles, every, LANES), f32),
+            pltpu.VMEM((3 * every, tiles * LANES), f32),
             dma((7,)),
             dma((2, half_ring, PIECES)),
             dma((2, half_ring, PIECES)),
@@ -425,7 +438,7 @@
             jax.ShapeDtypeStruct((ex, query_ids.shape[0]), f32),
         ),
         in_specs=[
-            pl.BlockSpec((tiles, every, LANES), lambda i: (0, 0, 0)),
+            pl.BlockSpec((3 * every, tiles * LANES), lambda i: (0, 0)),
             pl.BlockSpec((row_tiles, every, LANES), lambda i: (0, 0, 0)),
             pl.BlockSpec((every, LANES), lambda i: (0, 0)),
             smem,
@@ -435,12 +448,10 @@
             pl.BlockSpec((ex, query_ids.shape[0]), lambda i: (0, 0)),
         ),
         scratch_shapes=[
-            pltpu.VMEM((3 * every, tiles * LANES), bf16),
-            pltpu.VMEM((3 * every, tiles * LANES), f32),
             pltpu.VMEM((3 * every, LANES), f32),
             pltpu.SMEM((1,), f32),
         ],
-    )(cols, rows, inner, query_ids)
+    )(rhs, rows, inner, query_ids)
     return gram, scores.T
 
 

time: 149 us -> 148 us (level)
    pallas_call x1, Pallas kernels: 145 us -> 143 us  [body(): pl.pallas_call(functools.partial(kernel, n, nt), out_shape=(jax.ShapeDtyp...]
where the time goes in v3:
time: 148 us; the launch traced here: 147 us
  Pallas kernels  147 us (99%)
    pallas_call x1, Pallas kernels, body(): pl.pallas_call(functools.partial(kernel, n, nt), out_shape=(jax.ShapeDtyp...  143 us
    pallas_call x1, Pallas kernels, body(): pl.pallas_call(finish, grid=(row_tiles,), out_shape=(jax.ShapeDtypeStruct...  3.73 us

profile of v3, /device:TPU:6, one launch (start us, length us, event | category | flops | bytes accessed | tf_op | source)
XLA Modules:
  0.0 147.5 jit_solution(14568728616793170769)
XLA Ops:
  0.6 143.1 %shard_map.104 = (bf16[72,1024]{1,0:T(8,128)(2,1)}, f32[4,24,128]{2,1,0:T(8,128)}, f32[24,128]{1,0:T(8,128)}) custom-call(bf16[384,1024]{1,0:T(8,128)(2,1)} %acts.1, bf16[384,1024]{1,0:T(8,128)(2,1)} %grad.1, bf16[384,3584]{1,0:T(8,128)(2,1)} %gate.1, bf16[384,3584]{1,0:T(8,128)(2,1)} %up.1, bf16[3584,512]{1,0:T(8,128)(2,1)} %weight.1, ...), custom_call_target="tpu_custom_call" | custom-call | tf_op jit(solution)/shard_map/pallas_call | solution.py:391
  143.7 3.7 %shard_map.105 = (f32[512,1024]{1,0:T(8,128)}, f32[3,16]{1,0:T(4,128)}) custom-call(bf16[72,1024]{1,0:T(8,128)(2,1)} %get-tuple-element.7.rhs, f32[4,24,128]{2,1,0:T(8,128)} %get-tuple-element.8.rbuf, f32[24,128]{1,0:T(8,128)} %get-tuple-element.9.inner, s32[16]{0:T(128)} %query_ids.1), custom_call_target="tpu_custom_call" | custom-call | tf_op jit(solution)/shard_map/pallas_call | solution.py:433
